TPU v7x, 32 devices: a whole 2x2x4 slice. The times are simulated.
32 devices in a mesh: dp: 2 (over y), table: 16 (over z, x, core).
Axes of the slice: x: 2, y: 2, z: 4, core: 2. Of those that a mesh axis runs over, the one named last changes fastest.
Arguments:
- gradients: bfloat16 [256, 4096], P(None, ('dp', 'table')), may hold values from -16 to 16
- row_ids: int32 [4096], P(('dp', 'table')), may hold values from 0 to 32767
- table_block: float32 [256, 32768], P('table', 'dp'), may hold values from -6 to 6
- adagrad_state: float32 [32768], P('dp'), may hold values from 0.05 to 2
Outputs:
- new_table: float32 [256, 32768], P('table', 'dp')
- new_state: float32 [32768], P('dp')
All inputs are finite; a program needn't handle non-finite values.
Results may differ from a plain program's by a relative error of at most 0.0003.
Values may be sent and summed in bfloat16 or wider, within the bound.
A program may use at most 64 MiB of HBM per device.

v0:
```python
import jax
import jax.numpy as jnp
from jax import lax
from jax.sharding import PartitionSpec as P

W = 256
learn_rate = 0.5


def accumulate(grads, ids, first_row, count_rows):
    relative = ids - first_row
    inside = (relative >= 0) & (relative < count_rows)
    target = jnp.where(inside, relative, count_rows)
    start_total = jnp.zeros((grads.shape[0], count_rows), jnp.float32)
    return start_total.at[:, target].add(grads.astype(jnp.float32), mode="drop")


def body(gradients, row_ids, table_block, adagrad_state):
    owned = lax.all_to_all(gradients, "table", split_axis=0, concat_axis=1, tiled=True)
    local_rows = table_block.shape[1]
    all_row_ids = lax.all_gather(row_ids, ("dp", "table"), axis=0, tiled=True)
    first_row = lax.axis_index("dp") * local_rows
    row_grad = accumulate(
        lax.all_gather(owned, "dp", axis=1, tiled=True), all_row_ids, first_row, local_rows
    )
    partial_squares = jnp.sum(row_grad * row_grad, axis=0)
    squares = lax.psum(partial_squares, "table")
    new_state = adagrad_state + squares / W
    new_table = table_block - learn_rate * row_grad / jnp.sqrt(new_state)[None, :]
    return (new_table, new_state)


def solution(mesh):
    in_specs = (P(None, ("dp", "table")), P(("dp", "table")), P("table", "dp"), P("dp"))
    out_specs = (P("table", "dp"), P("dp"))
    return jax.shard_map(body, mesh=mesh, in_specs=in_specs, out_specs=out_specs, check_vma=False)
```

profile of v0, /device:TPU:8, one launch (start us, length us, event | category | flops | bytes accessed | tf_op | source)
XLA Modules:
  0.0 214.5 jit_solution(18062439507933522561)
XLA Ops:
  7.2 6.3 %all-to-all-start = ((bf16[16,16,128]{2,1,0:T(8,128)(2,1)}), bf16[16,16,128]{2,1,0:T(8,128)(2,1)S(1)}, u32[]{:S(2)}, u32[]{:S(2)}) async-start(bf16[16,16,128]{2,1,0:T(8,128)(2,1)} %bitcast.12), calls=%async_computation | async-start | bytes 131072 | tf_op jit(solution)/shard_map/all_to_all | solution.py:19
  13.4 0.0 all-reduce.2.cloned.1.call-start
  13.5 38.0 %all-gather = s32[32,1,128]{2,1,0:T(1,128)S(1)} all-gather(s32[1,1,128]{2,1,0:T(1,128)} %bitcast.15), channel_id=1, replica_groups=mesh['dp'=2,'table'=16] {'dp','table'}, dimensions={0}, use_global_device_ids=true | all-gather | bytes 16896 | tf_op jit(solution)/shard_map/all_gather | solution.py:21
  51.5 0.0 all-to-all-done
  51.5 0.3 copy.9
  51.8 14.8 %all_gather.7 = bf16[16,4096]{0,1:T(8,128)(2,1)S(1)} all-gather(bf16[16,2048]{0,1:T(8,128)(2,1)S(1)} %bitcast.10), channel_id=1, replica_groups=mesh['dp'=2,'table'=16] {'dp'}, dimensions={1}, use_global_device_ids=true | all-gather | bytes 196608 | tf_op jit(solution)/shard_map/all_gather | solution.py:24
  66.7 0.0 copy-start
  66.7 26.1 %scatter_custom_fusion = f32[16,16384]{0,1:T(8,128)} fusion(s32[4096]{0:T(1024)S(1)} %compare_select_fusion, f32[]{:T(128)} %constant.7.clone.1, bf16[16,4096]{0,1:T(8,128)(2,1)S(1)} %all_gather.7), kind=kCustom, calls=%fused_computation.3 | custom fusion | flops 131072 | bytes 2097156 | tf_op jit(solution)/shard_map/scatter-add | solution.py:15
  92.8 0.0 copy-start.1
  92.8 5.3 %multiply_reduce_fusion = f32[16384]{0:T(1024)} fusion(f32[16,16384]{0,1:T(8,128)} %scatter_custom_fusion), kind=kLoop, calls=%fused_computation.2 | loop fusion | flops 507904 | bytes 1114112 | tf_op jit(solution)/shard_map/reduce_sum | solution.py:26
  98.1 0.0 all-reduce.2.cloned.1.call-update
  98.1 0.0 copy-done
  98.1 4.6 %copy.10 = f32[16,16384]{0,1:T(8,128)} copy(f32[16,16384]{1,0:T(8,128)S(1)} %copy-done) | data formatting | bytes 2097152 | tf_op args[2]
  102.7 84.2 %all-reduce.2.cloned.1.call-done = f32[16384]{0:T(1024)} async-done(((f32[16384]{0:T(1024)}), f32[16384]{0:T(1024)}) %all-reduce.2.cloned.1.call-update) | async-done | bytes 65552 | tf_op jit(solution)/shard_map/psum | solution.py:27
  186.9 0.0 copy-done.1
  186.9 1.5 fusion.4
  188.4 13.3 %divide_subtract_fusion = f32[16,16384]{0,1:T(8,128)} fusion(f32[16,16384]{0,1:T(8,128)} %copy.10, f32[16,16384]{0,1:T(8,128)} %scatter_custom_fusion, f32[16384]{0:T(1024)S(1)} %get-tuple-element.6), kind=kLoop, calls=%fused_computation.1 | loop fusion | flops 786432 | bytes 3211264 | tf_op jit(solution)/shard_map/sub | solution.py:29
  201.7 6.0 %copy.11 = f32[16,16384]{1,0:T(8,128)} copy(f32[16,16384]{0,1:T(8,128)} %divide_subtract_fusion) | data formatting | bytes 2097152
  (2 shorter events, 0.0 us)
Async XLA Ops:
  7.2 44.4 %all-to-all-start = ((bf16[16,16,128]{2,1,0:T(8,128)(2,1)}), bf16[16,16,128]{2,1,0:T(8,128)(2,1)S(1)}, u32[]{:S(2)}, u32[]{:S(2)}) async-start(bf16[16,16,128]{2,1,0:T(8,128)(2,1)} %bitcast.12), calls=%async_computation | async-start | bytes 131072 | tf_op jit(solution)/shard_map/all_to_all | solution.py:19
  13.4 173.5 %all-reduce.2.cloned.1.call-start = ((), (), s32[]{:S(2)}) async-start(), calls=%async_computation.1 | async-start | bytes 131072 | tf_op jit(solution)/shard_map/psum | solution.py:27
  66.7 31.4 %copy-start = (f32[16,16384]{1,0:T(8,128)S(1)}, f32[16,16384]{1,0:T(8,128)}, u32[]{:S(2)}) copy-start(f32[16,16384]{1,0:T(8,128)} %param.6) | copy-start | bytes 3145732
  92.8 94.1 %copy-start.1 = (f32[16384]{0:T(1024)S(1)}, f32[16384]{0:T(1024)}, u32[]{:S(2)}) copy-start(f32[16384]{0:T(1024)} %param.7) | copy-start | bytes 196612
Sparse Core Ops, SparseCore 0:
  98.2 88.6 all-reduce.1
where the time goes:
time: 215 us
  waiting for transfers between devices  84.2 us (39%)
  blocking collectives  52.9 us (25%)
  other arithmetic  46.2 us (21%)
  between operations  14.1 us (7%)
  local copies, waits for them, and re-layouts  10.9 us (5%)
  starting transfers between devices  6.32 us (3%)
    psum x1, waiting for transfers between devices, body(): squares = lax.psum(partial_squares, 'table')  84.2 us
    all_gather x1, blocking collectives, body(): all_row_ids = lax.all_gather(row_ids, ('dp', 'table'), axis=0, tiled=True)  38 us
    scatter-add x1, other arithmetic, accumulate(): return start_total.at[:, target].add(grads.astype(jnp.float32), mode='drop')  26.1 us
    all_gather x1, blocking collectives, body(): lax.all_gather(owned, 'dp', axis=1, tiled=True)  14.8 us
    sub x1, other arithmetic, body(): table_block - learn_rate * row_grad / jnp.sqrt(new_state)[None, :]  13.3 us
    unnamed x6, local copies, waits for them, and re-layouts  10.6 us
    all_to_all x1, starting transfers between devices, body(): lax.all_to_all(gradients, 'table', split_axis=0, concat_axis=1, tiled=True)  6.28 us
    reduce_sum x1, other arithmetic, body(): partial_squares = jnp.sum(row_grad * row_grad, axis=0)  5.28 us
  transfers between devices with their start and end apart: 2, of which 1 were waited for; matrix products, arithmetic and copies ran while one was open for 2% of the time, Pallas kernels for 0%

commit v1 on v0

--- a/solution.py
+++ b/solution.py
@@ -24,7 +24,7 @@
         lax.all_gather(owned, "dp", axis=1, tiled=True), all_row_ids, first_row, local_rows
     )
     partial_squares = jnp.sum(row_grad * row_grad, axis=0)
-    squares = lax.psum(partial_squares, "table")
+    squares = jnp.sum(lax.all_gather(partial_squares, "table"), axis=0)
     new_state = adagrad_state + squares / W
     new_table = table_block - learn_rate * row_grad / jnp.sqrt(new_state)[None, :]
     return (new_table, new_state)

time: 215 us -> 166 us (0.77); the launches traced: 215 us -> 163 us
  waiting for transfers between devices: 84.2 us -> 32.2 us
    psum x1 -> x0, waiting for transfers between devices: 84.2 us -> none  [body(): squares = lax.psum(partial_squares, 'table')]
    all_gather x0 -> x1, waiting for transfers between devices: none -> 32.2 us  [body(): squares = jnp.sum(lax.all_gather(partial_squares, 'table'), axis=0)]
  transfers between devices with their start and end apart: 2 -> 2, of which waited for: 1 -> 1; matrix products, arithmetic and copies ran while one was open for 2% -> 3% of each run, Pallas kernels for 0% -> 0%
where the time goes in v1:
time: 166 us; the launch traced here: 163 us
  blocking collectives  52.9 us (32%)
  other arithmetic  45.5 us (27%)
  waiting for transfers between devices  32.2 us (19%)
  between operations  14.1 us (8%)
  local copies, waits for them, and re-layouts  12.3 us (7%)
  starting transfers between devices  6.32 us (4%)
    all_gather x1, blocking collectives, body(): all_row_ids = lax.all_gather(row_ids, ('dp', 'table'), axis=0, tiled=True)  38 us
    all_gather x1, waiting for transfers between devices, body(): squares = jnp.sum(lax.all_gather(partial_squares, 'table'), axis=0)  32.2 us
    scatter-add x1, other arithmetic, accumulate(): return start_total.at[:, target].add(grads.astype(jnp.float32), mode='drop')  26.1 us
    all_gather x1, blocking collectives, body(): lax.all_gather(owned, 'dp', axis=1, tiled=True)  14.8 us
    sub x1, other arithmetic, body(): table_block - learn_rate * row_grad / jnp.sqrt(new_state)[None, :]  13.3 us
    unnamed x6, local copies, waits for them, and re-layouts  10.6 us
    all_to_all x1, starting transfers between devices, body(): lax.all_to_all(gradients, 'table', split_axis=0, concat_axis=1, tiled=True)  6.28 us
    reduce_sum x1, other arithmetic, body(): partial_squares = jnp.sum(row_grad * row_grad, axis=0)  5.25 us
  transfers between devices with their start and end apart: 2, of which 1 were waited for; matrix products, arithmetic and copies ran while one was open for 3% of the time, Pallas kernels for 0%

profile of v1, /device:TPU:8, one launch (start us, length us, event | category | flops | bytes accessed | tf_op | source)
XLA Modules:
  0.0 163.3 jit_solution(18394290371067912784)
XLA Ops:
  7.2 6.3 %all-to-all-start = ((bf16[16,16,128]{2,1,0:T(8,128)(2,1)}), bf16[16,16,128]{2,1,0:T(8,128)(2,1)S(1)}, u32[]{:S(2)}, u32[]{:S(2)}) async-start(bf16[16,16,128]{2,1,0:T(8,128)(2,1)} %bitcast.12), calls=%async_computation | async-start | bytes 131072 | tf_op jit(solution)/shard_map/all_to_all | solution.py:19
  13.4 0.0 all-gather.4.cloned.1.call-start
  13.5 38.0 %all-gather.1 = s32[32,1,128]{2,1,0:T(1,128)S(1)} all-gather(s32[1,1,128]{2,1,0:T(1,128)} %bitcast.15), channel_id=1, replica_groups=mesh['dp'=2,'table'=16] {'dp','table'}, dimensions={0}, use_global_device_ids=true | all-gather | bytes 16896 | tf_op jit(solution)/shard_map/all_gather | solution.py:21
  51.5 0.0 all-to-all-done
  51.5 0.3 copy.12
  51.8 14.8 %all_gather.13 = bf16[16,4096]{0,1:T(8,128)(2,1)S(1)} all-gather(bf16[16,2048]{0,1:T(8,128)(2,1)S(1)} %bitcast.10), channel_id=1, replica_groups=mesh['dp'=2,'table'=16] {'dp'}, dimensions={1}, use_global_device_ids=true | all-gather | bytes 196608 | tf_op jit(solution)/shard_map/all_gather | solution.py:24
  66.7 0.0 copy-start
  66.7 26.1 %scatter_custom_fusion = f32[16,16384]{0,1:T(8,128)} fusion(s32[4096]{0:T(1024)S(1)} %compare_select_fusion, f32[]{:T(128)} %constant.7.clone.1, bf16[16,4096]{0,1:T(8,128)(2,1)S(1)} %all_gather.13), kind=kCustom, calls=%fused_computation.3 | custom fusion | flops 131072 | bytes 2097156 | tf_op jit(solution)/shard_map/scatter-add | solution.py:15
  92.8 5.3 %multiply_reduce_fusion = f32[16384]{0:T(1024)} fusion(f32[16,16384]{0,1:T(8,128)} %scatter_custom_fusion), kind=kLoop, calls=%fused_computation.2 | loop fusion | flops 507904 | bytes 1114112 | tf_op jit(solution)/shard_map/reduce_sum | solution.py:26
  98.0 0.0 copy-start.1
  98.0 0.0 all-gather.4.cloned.1.call-update
  98.1 0.0 copy-done
  98.1 4.6 %copy.13 = f32[16,16384]{0,1:T(8,128)} copy(f32[16,16384]{1,0:T(8,128)S(1)} %copy-done) | data formatting | bytes 2097152 | tf_op args[2]
  102.7 32.2 %all-gather.4.cloned.1.call-done = f32[262144]{0:T(1024)} async-done(((f32[16384]{0:T(1024)}), f32[262144]{0:T(1024)}) %all-gather.4.cloned.1.call-update) | async-done | bytes 1048592 | tf_op jit(solution)/shard_map/all_gather | solution.py:27
  134.9 1.4 reshape.16
  136.4 0.2 reduce_sum.19
  136.5 0.0 copy-done.1
  136.5 0.6 fusion.4
  137.2 13.3 %divide_subtract_fusion = f32[16,16384]{0,1:T(8,128)} fusion(f32[16,16384]{0,1:T(8,128)} %copy.13, f32[16,16384]{0,1:T(8,128)} %scatter_custom_fusion, f32[16384]{0:T(1024)S(1)} %get-tuple-element.8), kind=kLoop, calls=%fused_computation.1 | loop fusion | flops 786432 | bytes 3211264 | tf_op jit(solution)/shard_map/sub | solution.py:29
  150.5 6.0 %copy.14 = f32[16,16384]{1,0:T(8,128)} copy(f32[16,16384]{0,1:T(8,128)} %divide_subtract_fusion) | data formatting | bytes 2097152
  (2 shorter events, 0.0 us)
Async XLA Ops:
  7.2 44.4 %all-to-all-start = ((bf16[16,16,128]{2,1,0:T(8,128)(2,1)}), bf16[16,16,128]{2,1,0:T(8,128)(2,1)S(1)}, u32[]{:S(2)}, u32[]{:S(2)}) async-start(bf16[16,16,128]{2,1,0:T(8,128)(2,1)} %bitcast.12), calls=%async_computation | async-start | bytes 131072 | tf_op jit(solution)/shard_map/all_to_all | solution.py:19
  13.4 121.5 %all-gather.4.cloned.1.call-start = ((), (), s32[]{:S(2)}) async-start(), calls=%async_computation.1 | async-start | bytes 1114112 | tf_op jit(solution)/shard_map/all_gather | solution.py:27
  66.7 31.4 %copy-start = (f32[16,16384]{1,0:T(8,128)S(1)}, f32[16,16384]{1,0:T(8,128)}, u32[]{:S(2)}) copy-start(f32[16,16384]{1,0:T(8,128)} %param.6) | copy-start | bytes 3145732
  98.0 38.5 %copy-start.1 = (f32[16384]{0:T(1024)S(1)}, f32[16384]{0:T(1024)}, u32[]{:S(2)}) copy-start(f32[16384]{0:T(1024)} %param.7) | copy-start | bytes 196612
Sparse Core Ops, SparseCore 0:
  98.2 36.7 all-gather.3

commit v2 on v0

--- a/solution.py
+++ b/solution.py
@@ -21,7 +21,7 @@
     all_row_ids = lax.all_gather(row_ids, ("dp", "table"), axis=0, tiled=True)
     first_row = lax.axis_index("dp") * local_rows
     row_grad = accumulate(
-        lax.all_gather(owned, "dp", axis=1, tiled=True), all_row_ids, first_row, local_rows
+        jnp.concatenate(lax.all_gather(owned, "dp"), axis=1), all_row_ids, first_row, local_rows
     )
     partial_squares = jnp.sum(row_grad * row_grad, axis=0)
     squares = lax.psum(partial_squares, "table")

time: 215 us -> 205 us (0.953)
  blocking collectives: 52.9 us -> 43 us
    all_gather x1, blocking collectives: 14.8 us -> 5 us  [body(): lax.all_gather(owned, 'dp')]
where the time goes in v2:
time: 205 us
  waiting for transfers between devices  84.2 us (41%)
  other arithmetic  46.1 us (22%)
  blocking collectives  43 us (21%)
  between operations  14.1 us (7%)
  local copies, waits for them, and re-layouts  11.3 us (6%)
  starting transfers between devices  6.32 us (3%)
    psum x1, waiting for transfers between devices, body(): squares = lax.psum(partial_squares, 'table')  84.2 us
    all_gather x1, blocking collectives, body(): all_row_ids = lax.all_gather(row_ids, ('dp', 'table'), axis=0, tiled=True)  38 us
    scatter-add x1, other arithmetic, accumulate(): return start_total.at[:, target].add(grads.astype(jnp.float32), mode='drop')  26.1 us
    sub x1, other arithmetic, body(): table_block - learn_rate * row_grad / jnp.sqrt(new_state)[None, :]  13.3 us
    unnamed x6, local copies, waits for them, and re-layouts  10.6 us
    all_to_all x1, starting transfers between devices, body(): lax.all_to_all(gradients, 'table', split_axis=0, concat_axis=1, tiled=True)  6.28 us
    reduce_sum x1, other arithmetic, body(): partial_squares = jnp.sum(row_grad * row_grad, axis=0)  5.28 us
    all_gather x1, blocking collectives, body(): lax.all_gather(owned, 'dp')  5 us
  transfers between devices with their start and end apart: 2, of which 1 were waited for; matrix products, arithmetic and copies ran while one was open for 2% of the time, Pallas kernels for 0%

profile of v2, /device:TPU:8, one launch (start us, length us, event | category | flops | bytes accessed | tf_op | source)
XLA Modules:
  0.0 205.1 jit_solution(8947581150993282259)
XLA Ops:
  7.2 6.3 %all-to-all-start = ((bf16[16,16,128]{2,1,0:T(8,128)(2,1)}), bf16[16,16,128]{2,1,0:T(8,128)(2,1)S(1)}, u32[]{:S(2)}, u32[]{:S(2)}) async-start(bf16[16,16,128]{2,1,0:T(8,128)(2,1)} %bitcast.14), calls=%async_computation | async-start | bytes 131072 | tf_op jit(solution)/shard_map/all_to_all | solution.py:19
  13.4 0.0 all-reduce.2.cloned.1.call-start
  13.5 38.0 %all-gather = s32[32,1,128]{2,1,0:T(1,128)S(1)} all-gather(s32[1,1,128]{2,1,0:T(1,128)} %bitcast.17), channel_id=1, replica_groups=mesh['dp'=2,'table'=16] {'dp','table'}, dimensions={0}, use_global_device_ids=true | all-gather | bytes 16896 | tf_op jit(solution)/shard_map/all_gather | solution.py:21
  51.5 0.0 all-to-all-done
  51.6 5.0 %all_gather.11 = bf16[2,16,2048]{2,1,0:T(8,128)(2,1)S(1)} all-gather(bf16[1,16,2048]{2,1,0:T(8,128)(2,1)S(1)} %all_gather.10), channel_id=1, replica_groups=mesh['dp'=2,'table'=16] {'dp'}, dimensions={0}, use_global_device_ids=true | all-gather | bytes 196608 | tf_op jit(solution)/shard_map/all_gather | solution.py:24
  56.7 0.6 copy.18
  57.3 0.0 copy-start
  57.3 26.1 %scatter_custom_fusion = f32[16,16384]{0,1:T(8,128)} fusion(s32[4096]{0:T(1024)S(1)} %compare_select_fusion, f32[4096,16]{1,0:T(8,128)S(1)} %copy.18, f32[]{:T(128)} %constant.7.clone.1), kind=kCustom, calls=%fused_computation.3 | custom fusion | flops 65536 | bytes 1048580 | tf_op jit(solution)/shard_map/scatter-add | solution.py:15
  83.3 0.0 copy-start.1
  83.4 5.3 %multiply_reduce_fusion = f32[16384]{0:T(1024)} fusion(f32[16,16384]{0,1:T(8,128)} %scatter_custom_fusion), kind=kLoop, calls=%fused_computation.2 | loop fusion | flops 507904 | bytes 1114112 | tf_op jit(solution)/shard_map/reduce_sum | solution.py:26
  88.6 0.0 all-reduce.2.cloned.1.call-update
  88.7 0.0 copy-done
  88.7 4.6 %copy.19 = f32[16,16384]{0,1:T(8,128)} copy(f32[16,16384]{1,0:T(8,128)S(1)} %copy-done) | data formatting | bytes 2097152 | tf_op args[2]
  93.3 84.2 %all-reduce.2.cloned.1.call-done = f32[16384]{0:T(1024)} async-done(((f32[16384]{0:T(1024)}), f32[16384]{0:T(1024)}) %all-reduce.2.cloned.1.call-update) | async-done | bytes 65552 | tf_op jit(solution)/shard_map/psum | solution.py:27
  177.5 0.0 copy-done.1
  177.5 1.5 fusion.2
  179.0 13.3 %divide_subtract_fusion = f32[16,16384]{0,1:T(8,128)} fusion(f32[16,16384]{0,1:T(8,128)} %copy.19, f32[16,16384]{0,1:T(8,128)} %scatter_custom_fusion, f32[16384]{0:T(1024)S(1)} %get-tuple-element.10), kind=kLoop, calls=%fused_computation.1 | loop fusion | flops 786432 | bytes 3211264 | tf_op jit(solution)/shard_map/sub | solution.py:29
  192.2 6.0 %copy.20 = f32[16,16384]{1,0:T(8,128)} copy(f32[16,16384]{0,1:T(8,128)} %divide_subtract_fusion) | data formatting | bytes 2097152
  (6 shorter events, 0.1 us)
Async XLA Ops:
  7.2 44.4 %all-to-all-start = ((bf16[16,16,128]{2,1,0:T(8,128)(2,1)}), bf16[16,16,128]{2,1,0:T(8,128)(2,1)S(1)}, u32[]{:S(2)}, u32[]{:S(2)}) async-start(bf16[16,16,128]{2,1,0:T(8,128)(2,1)} %bitcast.14), calls=%async_computation | async-start | bytes 131072 | tf_op jit(solution)/shard_map/all_to_all | solution.py:19
  13.4 164.0 %all-reduce.2.cloned.1.call-start = ((), (), s32[]{:S(2)}) async-start(), calls=%async_computation.1 | async-start | bytes 131072 | tf_op jit(solution)/shard_map/psum | solution.py:27
  57.3 31.4 %copy-start = (f32[16,16384]{1,0:T(8,128)S(1)}, f32[16,16384]{1,0:T(8,128)}, u32[]{:S(2)}) copy-start(f32[16,16384]{1,0:T(8,128)} %param.6) | copy-start | bytes 3145732
  83.3 94.1 %copy-start.1 = (f32[16384]{0:T(1024)S(1)}, f32[16384]{0:T(1024)}, u32[]{:S(2)}) copy-start(f32[16384]{0:T(1024)} %param.7) | copy-start | bytes 196612
Sparse Core Ops, SparseCore 0:
  88.8 88.6 all-reduce.1
